TPU v7x, 512 devices: a whole 4x4x16 slice. The times are simulated.
512 devices in a mesh: rep: 4 (over x), tm: 16 (over z), height: 8 (over y, core).
Axes of the slice: x: 4, y: 4, z: 16, core: 2. Of those that a mesh axis runs over, the one named last changes fastest.
Arguments:
- inputs: bfloat16 [4, 64, 128, 32, 128], P('rep', 'tm', 'height'), may hold values from -32 to 32
- spatial_kernel: bfloat16 [3, 3, 128, 128], replicated, may hold values from -0.1875 to 0.1875
- temporal_kernel: bfloat16 [3, 128, 128], replicated, may hold values from -0.3125 to 0.3125
- norm_gain: float32 [128], replicated, may hold values from 0.1 to 1.9
- norm_shift: float32 [128], replicated, may hold values from -3 to 3
- cotangent: bfloat16 [4, 64, 128, 32, 128], P('rep', 'tm', 'height'), may hold values from -6 to 6
Outputs:
- outputs: bfloat16 [4, 64, 128, 32, 128], P('rep', 'tm', 'height')
- grad_inputs: bfloat16 [4, 64, 128, 32, 128], P('rep', 'tm', 'height')
- grad_spatial: float32 [3, 3, 128, 128], replicated
- grad_temporal: float32 [3, 128, 128], replicated
- grad_gain: float32 [128], replicated
- grad_shift: float32 [128], replicated
All inputs are finite; a program needn't handle non-finite values.
Results may differ from a plain program's by a relative error of at most 0.0041.
The roundings to bfloat16 on the way count: a program that leaves them out, or rounds other values in their place, can miss the bound.
Values may be sent and summed in bfloat16 or wider, within the bound.
No kernel may reach another device: no remote copies, remote signals or barrier semaphores. Data moves between devices by JAX's collectives and lax.ppermute only.
A program may use at most 64 MiB of HBM per device.

v0:
```python
import math
import jax
import jax.numpy as jnp
from jax import lax
from jax.sharding import PartitionSpec as P

GROUPS = 32
EPS = 1e-05


def with_halo(value, sides, width):
    for axis, dim in sides:
        count, length = (lax.axis_size(axis), value.shape[dim])
        up = [(i, (i + 1) % count) for i in range(count - 1)]
        down = [(j, i) for i, j in up]
        last = lax.slice_in_dim(value, length - width, length, axis=dim)
        first = lax.slice_in_dim(value, 0, width, axis=dim)
        before = lax.ppermute(last, axis, up)
        after = lax.ppermute(first, axis, down)
        value = jnp.concatenate([before, value, after], axis=dim)
    return value


def from_behind(value, axis, steps):
    count = lax.axis_size(axis)
    first, last = (max(0, -steps), min(count, count - steps))
    return lax.ppermute(value, axis, [(source, source + steps) for source in range(first, last)])


def carried_in(part, axis, combine, identity, reverse):
    count = lax.axis_size(axis)
    place = lax.axis_index(axis)
    ahead = count - 1 - place if reverse else place
    gathered = jax.tree.map(lambda a: lax.all_gather(a, axis), part)
    state = jax.tree.map(lambda a, e: jnp.zeros_like(a) + jnp.asarray(e, a.dtype), part, identity)

    def one(turn, state):
        source = count - 1 - turn if reverse else turn
        return combine(
            state, jax.tree.map(lambda a: lax.dynamic_index_in_dim(a, source, 0, False), gathered)
        )

    return lax.fori_loop(0, ahead, one, state)


def add_pair(earlier, later):
    return (earlier[0] + later[0], earlier[1] + later[1])


def reverse_sum(values):
    return jnp.cumsum(values[::-1], 0)[::-1]


def widen(stat):
    return stat[:, None, None, :, None]


def shards(inputs, spatial_kernel, temporal_kernel, norm_gain, norm_shift, cotangent):
    pixels_in = inputs[0]
    frames, rows, columns, channels = pixels_in.shape
    group_size = channels // GROUPS
    time_devices = lax.axis_size("tm")
    height_devices = lax.axis_size("height")
    frame_start = lax.axis_index("tm") * frames
    per_frame = float(rows * height_devices * columns * group_size)
    halo_in = with_halo(pixels_in, (("height", 1),), 1)
    padded = jnp.pad(halo_in, ((0, 0), (0, 0), (1, 1), (0, 0)))
    total = jnp.zeros((frames, rows, columns, channels), jnp.float32)
    for row_tap in range(3):
        for col_tap in range(3):
            window = padded[:, row_tap : row_tap + rows, col_tap : col_tap + columns]
            total = total + jnp.einsum(
                "frwc,cd->frwd",
                window,
                spatial_kernel[row_tap, col_tap],
                preferred_element_type=jnp.float32,
            )
    feature = total.astype(jnp.bfloat16)
    prior = from_behind(feature[frames - 2 :], "tm", 1)
    earlier = jnp.concatenate([prior, feature], 0)
    mixed = jnp.zeros((frames, rows, columns, channels), jnp.float32)
    for time_tap in range(3):
        mixed = mixed + jnp.einsum(
            "frwc,cd->frwd",
            earlier[time_tap : time_tap + frames],
            temporal_kernel[time_tap],
            preferred_element_type=jnp.float32,
        )
    grouped = mixed.reshape(frames, rows, columns, GROUPS, group_size)
    first = grouped.sum((1, 2, 4))
    second = (grouped * grouped).sum((1, 2, 4))
    row_first, row_second = lax.psum((first, second), "height")
    empty = jnp.zeros((GROUPS,), jnp.float32)
    before = carried_in(
        (row_first.sum(0), row_second.sum(0)), "tm", add_pair, (empty, empty), False
    )
    counted = ((frame_start + jnp.arange(frames)).astype(jnp.float32) + 1.0)[:, None] * per_frame
    mean = (before[0] + jnp.cumsum(row_first, 0)) / counted
    variance = (before[1] + jnp.cumsum(row_second, 0)) / counted - mean * mean
    inv_std = lax.rsqrt(variance + EPS)
    normed = (grouped - widen(mean)) * widen(inv_std)
    gain = norm_gain.reshape(GROUPS, group_size)
    shift = norm_shift.reshape(GROUPS, group_size)
    pre = normed * gain + shift
    sigma = jax.nn.sigmoid(pre)
    outputs = (
        pixels_in.astype(jnp.float32) + (pre * sigma).reshape(frames, rows, columns, channels)
    ).astype(jnp.bfloat16)
    grad_pre = cotangent[0].astype(jnp.float32).reshape(grouped.shape) * (
        sigma * (1.0 + pre * (1.0 - sigma))
    )
    gain_part = (grad_pre * normed).sum((0, 1, 2)).reshape(channels)
    shift_part = grad_pre.sum((0, 1, 2)).reshape(channels)
    grad_normed = grad_pre * gain
    local_a = grad_normed.sum((1, 2, 4))
    local_b = (grad_normed * normed).sum((1, 2, 4))
    sum_a, sum_b = lax.psum((local_a, local_b), "height")
    q_first = (-inv_std * sum_a + inv_std * inv_std * sum_b * mean) / counted
    q_second = -inv_std * inv_std * sum_b / (2.0 * counted)
    zeroed = jnp.zeros((GROUPS,), jnp.float32)
    after = carried_in((q_first.sum(0), q_second.sum(0)), "tm", add_pair, (zeroed, zeroed), True)
    carry_first = after[0] + reverse_sum(q_first)
    carry_second = after[1] + reverse_sum(q_second)
    grad_mixed = (
        widen(inv_std) * grad_normed + widen(carry_first) + 2.0 * grouped * widen(carry_second)
    )
    grad_mixed = grad_mixed.reshape(frames, rows, columns, channels).astype(jnp.bfloat16)
    temporal_terms = []
    for time_tap in range(3):
        temporal_terms.append(
            jnp.einsum(
                "frwc,frwd->cd",
                earlier[time_tap : time_tap + frames],
                grad_mixed,
                preferred_element_type=jnp.float32,
            )
        )
    temporal_part = jnp.stack(temporal_terms)
    following = from_behind(grad_mixed[:2], "tm", -1)
    later = jnp.concatenate([grad_mixed, following], 0)
    grad_feature = jnp.zeros((frames, rows, columns, channels), jnp.float32)
    for time_tap in range(3):
        grad_feature = grad_feature + jnp.einsum(
            "frwd,cd->frwc",
            later[2 - time_tap : 2 - time_tap + frames],
            temporal_kernel[time_tap],
            preferred_element_type=jnp.float32,
        )
    grad_feature = grad_feature.astype(jnp.bfloat16)
    halo_grad = with_halo(grad_feature, (("height", 1),), 1)
    padded_grad = jnp.pad(halo_grad, ((0, 0), (0, 0), (1, 1), (0, 0)))
    grad_in = cotangent[0].astype(jnp.float32)
    spatial_terms = []
    for row_tap in range(3):
        for col_tap in range(3):
            back = padded_grad[
                :, 2 - row_tap : 2 - row_tap + rows, 2 - col_tap : 2 - col_tap + columns
            ]
            grad_in = grad_in + jnp.einsum(
                "frwd,cd->frwc",
                back,
                spatial_kernel[row_tap, col_tap],
                preferred_element_type=jnp.float32,
            )
            window = padded[:, row_tap : row_tap + rows, col_tap : col_tap + columns]
            spatial_terms.append(
                jnp.einsum(
                    "frwc,frwd->cd", window, grad_feature, preferred_element_type=jnp.float32
                )
            )
    spatial_part = jnp.stack(spatial_terms).reshape(3, 3, channels, channels)
    grad_inputs = grad_in.astype(jnp.bfloat16)
    spatial_sum, temporal_sum, gain_sum, shift_sum = lax.psum(
        (spatial_part, temporal_part, gain_part, shift_part), ("rep", "tm", "height")
    )
    pixel_total = lax.axis_size("rep") * frames * time_devices * rows * height_devices * columns
    scale = 1.0 / math.sqrt(pixel_total)
    return (
        outputs[None],
        grad_inputs[None],
        spatial_sum * scale,
        temporal_sum * scale,
        gain_sum * scale,
        shift_sum * scale,
    )


def solution(mesh):
    in_specs = (
        P("rep", "tm", "height", None, None),
        P(),
        P(),
        P(),
        P(),
        P("rep", "tm", "height", None, None),
    )
    out_specs = (
        P("rep", "tm", "height", None, None),
        P("rep", "tm", "height", None, None),
        P(),
        P(),
        P(),
        P(),
    )
    return jax.shard_map(shards, mesh=mesh, in_specs=in_specs, out_specs=out_specs, check_vma=False)
```

profile of v0, /device:TPU:2, one launch (start us, length us, event | category | flops | bytes accessed | tf_op | source)
XLA Modules:
  0.0 734.6 jit_solution(1848081160454730432)
XLA Ops:
  7.2 0.8 fusion.138
  8.0 1.7 collective-permute-start
  9.8 1.3 collective-permute-start.1
  11.1 0.5 fusion.122
  11.6 0.5 fusion.121
  12.2 1.3 dynamic-slice
  14.2 1.4 select_maximum_fusion.2
  15.6 0.3 fusion.52
  15.9 0.7 copy-done
  17.2 0.3 convolution_add_fusion.10
  18.1 0.3 convolution_add_fusion.7
  19.0 3.8 collective-permute-start.2
  23.1 4.7 collective-permute-done.2
  28.1 0.9 multiply_reduce_fusion
  29.1 0.8 reduce_sum.101
  29.9 1.4 reduce_sum.123
  31.3 0.7 reduce_sum.120
  32.0 0.9 reduce_sum.124
  32.9 15.0 %all-reduce.11 = (f32[4,32]{1,0:T(4,128)S(1)}, f32[4,32]{1,0:T(4,128)S(1)}) all-reduce(f32[4,32]{1,0:T(4,128)} %reduce_sum.120, f32[4,32]{1,0:T(4,128)S(1)} %reduce_sum.124), channel_id=1, replica_groups=mesh['rep'=4,'tm'=16,'height'=8] {'height'}, use_global_device_ids=true, to_apply=%region_2.3 | all-reduce | flops 256 | bytes 2048 | tf_op jit(solution)/shard_map/psum | solution.py:92
  48.4 37.0 %all-reduce.9 = (f32[512]{0:T(512)S(1)}, f32[512]{0:T(512)S(1)}) all-reduce(f32[512]{0:T(512)S(1)} %dynamic-update-slice, f32[512]{0:T(512)S(1)} %dynamic-update-slice.1), channel_id=2, replica_groups=mesh['rep'=4,'tm'=16,'height'=8] {'tm'}, use_global_device_ids=true, to_apply=%add.2 | all-reduce | flops 1024 | bytes 8192
  85.7 1.3 add_rsqrt_fusion
  87.0 0.6 copy-done.12
  87.6 0.7 mul.190
  88.3 0.8 sub.44
  89.1 0.7 sub.45
  89.9 1.5 fusion.30
  91.8 12.4 %all-reduce.10 = (f32[4,32]{1,0:T(4,128)S(1)}, f32[4,32]{1,0:T(4,128)S(1)}) all-reduce(f32[4,32]{1,0:T(4,128)S(1)} %reduce_sum.131, f32[4,32]{1,0:T(4,128)S(1)} %reduce_sum.128), channel_id=1, replica_groups=mesh['rep'=4,'tm'=16,'height'=8] {'height'}, use_global_device_ids=true, to_apply=%region_17.18 | all-reduce | flops 256 | bytes 2048 | tf_op jit(solution)/shard_map/psum | solution.py:117
  104.8 28.7 %all-reduce.8 = (f32[512]{0:T(512)S(1)}, f32[512]{0:T(512)S(1)}) all-reduce(f32[512]{0:T(512)S(1)} %dynamic-update-slice.2, f32[512]{0:T(512)S(1)} %dynamic-update-slice.3), channel_id=4, replica_groups=mesh['rep'=4,'tm'=16,'height'=8] {'tm'}, use_global_device_ids=true, to_apply=%add.4 | all-reduce | flops 1024 | bytes 8192
  133.6 0.7 while.27
  134.9 2.7 fusion.28
  137.6 0.3 convolution_bitcast_fusion.4
  137.9 1.3 collective-permute-start.3
  139.2 99.2 %all-reduce.6 = (f32[128]{0:T(128)S(1)}, f32[128]{0:T(128)S(1)}) all-reduce(f32[128]{0:T(128)S(1)} %get-tuple-element.125, f32[128]{0:T(128)S(1)} %get-tuple-element.128), channel_id=1, replica_groups=mesh['rep'=4,'tm'=16,'height'=8] {'rep','tm','height'}, use_global_device_ids=true, to_apply=%region_27.28 | all-reduce | flops 256 | bytes 2048 | tf_op jit(solution)/shard_map/psum | solution.py:173
  238.4 0.5 broadcast_multiply_fusion.2
  239.0 0.3 convolution_bitcast_fusion.1
  239.3 0.3 convolution_bitcast_fusion
  239.6 0.7 pad_maximum_fusion.10
  240.6 1.2 fusion.50
  241.8 1.2 fusion.13
  243.1 0.3 fusion.23
  243.5 0.6 copy-done.4
  244.4 0.3 fusion.16
  244.7 0.3 fusion.22
  245.1 0.3 fusion.21
  245.4 0.3 fusion.20
  245.7 0.3 fusion.19
  246.1 0.3 fusion.18
  246.4 1.7 collective-permute-start.4
  248.2 1.3 collective-permute-start.5
  249.5 0.3 fusion.15
  249.8 0.3 fusion.17
  250.2 0.8 copy-done.7
  251.0 1.2 collective-permute-done.5
  252.2 0.3 select_maximum_fusion
  252.6 0.3 convolution_add_fusion.5
  252.9 0.3 fusion.40
  253.2 0.3 fusion.42
  253.5 0.3 fusion.44
  254.1 0.5 fusion.8
  254.7 0.3 fusion.38
  255.0 1.1 fusion.14
  256.1 469.0 %all-reduce.14.cloned.1.call-done = (f32[3,3,128,128]{3,2,1,0:T(8,128)}, f32[3,128,128]{2,1,0:T(8,128)}) async-done(((f32[3,3,128,128]{3,2,1,0:T(8,128)}, f32[3,128,128]{2,1,0:T(8,128)}), (f32[3,3,128,128]{3,2,1,0:T(8,128)}, f32[3,128,128]{2,1,0:T(8,128)})) %all-reduce.14.cloned.1.call-update) | async-done | bytes 786448 | tf_op jit(solution)/shard_map/psum | solution.py:173
  725.1 2.0 broadcast_multiply_fusion
  727.1 0.7 broadcast_multiply_fusion.1
  (111 shorter events, 6.2 us)
Async XLA Ops:
  7.2 8.4 %copy-start.3 = (bf16[3,3,128,128]{3,2,1,0:T(8,128)(2,1)S(1)}, bf16[3,3,128,128]{3,2,1,0:T(8,128)(2,1)}, u32[]{:S(2)}) copy-start(bf16[3,3,128,128]{3,2,1,0:T(8,128)(2,1)} %param.11) | copy-start | bytes 884740
  7.2 717.9 %all-reduce.14.cloned.1.call-start = ((), (), s32[]{:S(2)}) async-start(), calls=%async_computation | async-start | bytes 1572864 | tf_op jit(solution)/shard_map/psum | solution.py:173
  8.0 6.0 collective-permute-start
  9.8 4.5 collective-permute-start.1
  14.1 1.9 copy-start.10
  15.6 1.0 copy-start
  18.7 4.2 copy-start.8
  19.0 8.8 %collective-permute-start.2 = (bf16[2,16,32,128]{3,2,1,0:T(8,128)(2,1)S(1)}, bf16[2,16,32,128]{3,2,1,0:T(8,128)(2,1)S(1)}, u32[]{:S(2)}, u32[]{:S(2)}) collective-permute-start(bf16[2,16,32,128]{3,2,1,0:T(8,128)(2,1)S(1)} %slice.195), channel_id=1, source_target_pairs={{0,8},{8,16},{16,24},{24,32},{32,40},{40,48},{48,56},{56,64},{64,7... | collective-permute-start | bytes 786440 | tf_op jit(solution)/shard_map/ppermute | solution.py:27
  27.8 1.2 copy-start.5
  29.1 60.8 %copy-start.1 = (bf16[1,4,16,32,128]{4,3,2,1,0:T(8,128)(2,1)S(1)}, bf16[1,4,16,32,128]{4,3,2,1,0:T(8,128)(2,1)}, u32[]{:S(2)}) copy-start(bf16[1,4,16,32,128]{4,3,2,1,0:T(8,128)(2,1)} %param.15) | copy-start | bytes 1572868
  87.0 0.6 copy-start.12
  89.8 14.4 %copy-start.13 = (f32[4,32]{1,0:T(4,128)S(1)}, f32[4,32]{1,0:T(4,128)}, u32[]{:S(2)}) copy-start(f32[4,32]{1,0:T(4,128)} %copy-done.12) | copy-start | bytes 1540
  89.8 14.4 %copy-start.14 = (f32[4,32]{1,0:T(4,128)S(1)}, f32[4,32]{1,0:T(4,128)}, u32[]{:S(2)}) copy-start(f32[4,32]{1,0:T(4,128)} %get-tuple-element.172) | copy-start | bytes 1540
  89.8 14.4 %copy-start.19 = (f32[4]{0:T(128)S(1)}, f32[4]{0:T(128)}, u32[]{:S(2)}) copy-start(f32[4]{0:T(128)} %fusion.122) | copy-start | bytes 52
  89.8 14.4 %copy-start.20 = (f32[4]{0:T(128)S(1)}, f32[4]{0:T(128)}, u32[]{:S(2)}) copy-start(f32[4]{0:T(128)} %fusion.121) | copy-start | bytes 52
  89.8 45.0 %copy-start.15 = (f32[4,128]{1,0:T(4,128)S(1)}, f32[4,128]{1,0:T(4,128)}, u32[]{:S(2)}) copy-start(f32[4,128]{1,0:T(4,128)} %mul.190) | copy-start | bytes 6148
  89.8 45.0 %copy-start.16 = (f32[4,128]{1,0:T(4,128)S(1)}, f32[4,128]{1,0:T(4,128)}, u32[]{:S(2)}) copy-start(f32[4,128]{1,0:T(4,128)} %sub.45) | copy-start | bytes 6148
  89.9 45.0 %copy-start.17 = (f32[128]{0:T(128)S(1)}, f32[128]{0:T(128)}, u32[]{:S(2)}) copy-start(f32[128]{0:T(128)} %param.13) | copy-start | bytes 1540
  89.9 45.0 %copy-start.18 = (f32[128]{0:T(128)S(1)}, f32[128]{0:T(128)}, u32[]{:S(2)}) copy-start(f32[128]{0:T(128)} %param.14) | copy-start | bytes 1540
  137.6 101.4 %copy-start.6 = (bf16[2,16,32,128]{3,2,1,0:T(8,128)(2,1)S(1)}, bf16[2,16,32,128]{3,2,1,0:T(8,128)(2,1)}, u32[]{:S(2)}) copy-start(bf16[2,16,32,128]{3,2,1,0:T(8,128)(2,1)} %copy-done.5) | copy-start | bytes 786436
  137.9 102.7 %collective-permute-start.3 = (bf16[2,16,32,128]{3,2,1,0:T(8,128)(2,1)S(1)}, bf16[2,16,32,128]{3,2,1,0:T(8,128)(2,1)}, u32[]{:S(2)}, u32[]{:S(2)}) collective-permute-start(bf16[2,16,32,128]{3,2,1,0:T(8,128)(2,1)S(1)} %slice.196), channel_id=1, source_target_pairs={{8,0},{16,8},{24,16},{32,24},{40,32},{48,40},{56,48},{64,56},{72,6... | collective-permute-start | bytes 786440 | tf_op jit(solution)/shard_map/ppermute | solution.py:27
  243.1 1.0 copy-start.4
  243.5 0.9 copy-start.11
  246.4 4.6 collective-permute-start.4
  248.2 4.0 collective-permute-start.5
  250.2 0.8 copy-start.7
  251.0 1.6 copy-start.2
  725.1 2.0 copy-start.9
Sparse Core Ops, SparseCore 0:
  251.1 473.9 all-reduce.13
where the time goes:
time: 735 us
  waiting for transfers between devices  475 us (65%)
  blocking collectives  192 us (26%)
  between operations  15.2 us (2%)
  matrix products  14.7 us (2%)
  other arithmetic  14.4 us (2%)
  local copies, waits for them, and re-layouts  11.3 us (2%)
  starting transfers between devices  11.2 us (2%)
    psum x1, waiting for transfers between devices, shards(): lax.psum((spatial_part, temporal_part, gain_part, shift_part), ('rep', 't...  469 us
    psum x1, blocking collectives, shards(): lax.psum((spatial_part, temporal_part, gain_part, shift_part), ('rep', 't...  99.2 us
    unnamed x2, blocking collectives  65.7 us
    psum x1, blocking collectives, shards(): row_first, row_second = lax.psum((first, second), 'height')  15 us
  transfers between devices with their start and end apart: 7, of which 4 were waited for; matrix products, arithmetic and copies ran while one was open for 1% of the time, Pallas kernels for 0%

commit v1 on v0

--- a/solution.py
+++ b/solution.py
@@ -6,6 +6,12 @@
 
 GROUPS = 32
 EPS = 1e-05
+
+
+def lay_ticks_for(t0):
+    for it in ("rep", ("tm", "height")):
+        t0 = lax.psum(t0, it)
+    return t0
 
 
 def with_halo(value, sides, width):
@@ -170,8 +176,8 @@
             )
     spatial_part = jnp.stack(spatial_terms).reshape(3, 3, channels, channels)
     grad_inputs = grad_in.astype(jnp.bfloat16)
-    spatial_sum, temporal_sum, gain_sum, shift_sum = lax.psum(
-        (spatial_part, temporal_part, gain_part, shift_part), ("rep", "tm", "height")
+    spatial_sum, temporal_sum, gain_sum, shift_sum = lay_ticks_for(
+        (spatial_part, temporal_part, gain_part, shift_part)
     )
     pixel_total = lax.axis_size("rep") * frames * time_devices * rows * height_devices * columns
     scale = 1.0 / math.sqrt(pixel_total)

time: 735 us -> 817 us (1.11)
  blocking collectives: 192 us -> 348 us
  waiting for transfers between devices: 475 us -> 399 us
    psum x1 -> x2, blocking collectives: 99.2 us -> 255 us  [lay_ticks_for(): t0 = lax.psum(t0, it)]
    psum x1 -> x2, waiting for transfers between devices: 469 us -> 393 us  [lay_ticks_for(): t0 = lax.psum(t0, it)]
  transfers between devices with their start and end apart: 7 -> 8, of which waited for: 4 -> 5; matrix products, arithmetic and copies ran while one was open for 1% -> 1% of each run, Pallas kernels for 0% -> 0%
where the time goes in v1:
time: 817 us; the launch traced here: 816 us
  waiting for transfers between devices  399 us (49%)
  blocking collectives  348 us (43%)
  between operations  15.2 us (2%)
  other arithmetic  14.9 us (2%)
  matrix products  13.7 us (2%)
  local copies, waits for them, and re-layouts  13 us (2%)
  starting transfers between devices  11.5 us (1%)
    psum x2, waiting for transfers between devices, lay_ticks_for(): t0 = lax.psum(t0, it)  393 us
    psum x2, blocking collectives, lay_ticks_for(): t0 = lax.psum(t0, it)  255 us
    unnamed x2, blocking collectives  65.7 us
  transfers between devices with their start and end apart: 8, of which 5 were waited for; matrix products, arithmetic and copies ran while one was open for 1% of the time, Pallas kernels for 0%

profile of v1, /device:TPU:2, one launch (start us, length us, event | category | flops | bytes accessed | tf_op | source)
XLA Modules:
  0.0 815.8 jit_solution(8473787645335572052)
XLA Ops:
  7.2 0.8 fusion.138
  8.0 1.7 collective-permute-start
  9.8 1.3 collective-permute-start.1
  11.1 0.5 fusion.122
  11.6 0.5 fusion.121
  12.2 1.3 dynamic-slice
  14.2 1.4 select_maximum_fusion.2
  15.6 0.3 fusion.52
  15.9 0.7 copy-done
  17.2 0.3 convolution_add_fusion.10
  18.1 0.3 convolution_add_fusion.7
  19.0 3.8 collective-permute-start.2
  23.1 4.7 collective-permute-done.2
  28.1 0.9 multiply_reduce_fusion
  29.1 0.8 reduce_sum.101
  29.9 1.4 reduce_sum.123
  31.3 0.7 reduce_sum.120
  32.0 0.9 reduce_sum.124
  32.9 15.0 %all-reduce.11 = (f32[4,32]{1,0:T(4,128)S(1)}, f32[4,32]{1,0:T(4,128)S(1)}) all-reduce(f32[4,32]{1,0:T(4,128)} %reduce_sum.120, f32[4,32]{1,0:T(4,128)S(1)} %reduce_sum.124), channel_id=1, replica_groups=mesh['rep'=4,'tm'=16,'height'=8] {'height'}, use_global_device_ids=true, to_apply=%region_2.3 | all-reduce | flops 256 | bytes 2048 | tf_op jit(solution)/shard_map/psum | solution.py:98
  48.4 37.0 %all-reduce.9 = (f32[512]{0:T(512)S(1)}, f32[512]{0:T(512)S(1)}) all-reduce(f32[512]{0:T(512)S(1)} %dynamic-update-slice, f32[512]{0:T(512)S(1)} %dynamic-update-slice.1), channel_id=2, replica_groups=mesh['rep'=4,'tm'=16,'height'=8] {'tm'}, use_global_device_ids=true, to_apply=%add.2 | all-reduce | flops 1024 | bytes 8192
  85.7 1.3 add_rsqrt_fusion
  87.0 0.6 copy-done.13
  87.6 0.7 mul.190
  88.3 0.8 sub.44
  89.1 0.7 sub.45
  89.9 2.0 fusion.30
  92.3 12.4 %all-reduce.10 = (f32[4,32]{1,0:T(4,128)S(1)}, f32[4,32]{1,0:T(4,128)S(1)}) all-reduce(f32[4,32]{1,0:T(4,128)S(1)} %reduce_sum.131, f32[4,32]{1,0:T(4,128)S(1)} %reduce_sum.128), channel_id=1, replica_groups=mesh['rep'=4,'tm'=16,'height'=8] {'height'}, use_global_device_ids=true, to_apply=%region_17.18 | all-reduce | flops 256 | bytes 2048 | tf_op jit(solution)/shard_map/psum | solution.py:123
  105.3 28.7 %all-reduce.8 = (f32[512]{0:T(512)S(1)}, f32[512]{0:T(512)S(1)}) all-reduce(f32[512]{0:T(512)S(1)} %dynamic-update-slice.2, f32[512]{0:T(512)S(1)} %dynamic-update-slice.3), channel_id=4, replica_groups=mesh['rep'=4,'tm'=16,'height'=8] {'tm'}, use_global_device_ids=true, to_apply=%add.4 | all-reduce | flops 1024 | bytes 8192
  134.1 0.7 while.27
  135.4 2.7 fusion.28
  138.1 0.3 convolution_bitcast_fusion.4
  138.5 1.3 collective-permute-start.3
  139.8 8.6 %all-reduce.12 = (f32[128]{0:T(128)S(1)}, f32[128]{0:T(128)S(1)}) all-reduce(f32[128]{0:T(128)S(1)} %copy-done.21, f32[128]{0:T(128)S(1)} %copy-done.22), channel_id=1, replica_groups=mesh['rep'=4,'tm'=16,'height'=8] {'rep'}, use_global_device_ids=true, to_apply=%region_29.30 | all-reduce | flops 256 | bytes 2048 | tf_op jit(solution)/shard_map/psum | solution.py:13
  148.4 246.8 %all-reduce.6 = (f32[128]{0:T(128)S(1)}, f32[128]{0:T(128)S(1)}) all-reduce(f32[128]{0:T(128)S(1)} %get-tuple-element.167, f32[128]{0:T(128)S(1)} %get-tuple-element.168), channel_id=1, replica_groups=mesh['rep'=4,'tm'=16,'height'=8] {'tm','height'}, use_global_device_ids=true, to_apply=%region_30.31 | all-reduce | flops 256 | bytes 2048 | tf_op jit(solution)/shard_map/psum | solution.py:13
  395.2 0.5 broadcast_multiply_fusion.2
  395.7 0.3 convolution_bitcast_fusion.1
  396.0 0.3 convolution_bitcast_fusion
  396.4 0.7 pad_maximum_fusion.10
  398.0 0.3 fusion.23
  398.4 0.6 copy-done.5
  398.9 1.3 fusion.73
  400.2 0.3 fusion.16
  400.6 0.3 fusion.22
  400.9 0.3 fusion.21
  401.3 0.3 fusion.20
  401.6 0.3 fusion.19
  402.0 0.3 fusion.18
  402.3 1.8 collective-permute-start.4
  404.1 1.5 collective-permute-start.5
  405.6 0.3 fusion.15
  405.9 0.3 fusion.17
  406.3 0.8 copy-done.8
  407.4 0.3 select_maximum_fusion
  407.7 0.3 fusion.40
  408.3 0.3 fusion.44
  409.0 0.7 copy-done.2
  409.7 0.3 convolution_add_fusion.5
  410.0 0.9 copy-done.3
  410.9 0.5 fusion.8
  411.4 51.0 %all-reduce.19.cloned.1.call-done = (f32[3,3,128,128]{3,2,1,0:T(8,128)}, f32[3,128,128]{2,1,0:T(8,128)}) async-done(((f32[3,3,128,128]{3,2,1,0:T(8,128)}, f32[3,128,128]{2,1,0:T(8,128)}), (f32[3,3,128,128]{3,2,1,0:T(8,128)}, f32[3,128,128]{2,1,0:T(8,128)})) %all-reduce.19.cloned.1.call-update) | async-done | bytes 786448 | tf_op jit(solution)/shard_map/psum | solution.py:13
  462.7 1.1 fusion.14
  463.8 342.5 %all-reduce.17.cloned.1.call-done = (f32[3,3,128,128]{3,2,1,0:T(8,128)}, f32[3,128,128]{2,1,0:T(8,128)}) async-done(((f32[3,3,128,128]{3,2,1,0:T(8,128)}, f32[3,128,128]{2,1,0:T(8,128)}), (f32[3,3,128,128]{3,2,1,0:T(8,128)}, f32[3,128,128]{2,1,0:T(8,128)})) %all-reduce.17.cloned.1.call-update) | async-done | bytes 786448 | tf_op jit(solution)/shard_map/psum | solution.py:13
  806.3 2.0 broadcast_multiply_fusion
  808.3 0.7 broadcast_multiply_fusion.1
  (121 shorter events, 7.4 us)
Async XLA Ops:
  7.2 8.4 %copy-start.4 = (bf16[3,3,128,128]{3,2,1,0:T(8,128)(2,1)S(1)}, bf16[3,3,128,128]{3,2,1,0:T(8,128)(2,1)}, u32[]{:S(2)}) copy-start(bf16[3,3,128,128]{3,2,1,0:T(8,128)(2,1)} %param.11) | copy-start | bytes 884740
  7.2 455.2 %all-reduce.19.cloned.1.call-start = ((), (), s32[]{:S(2)}) async-start(), calls=%async_computation.1 | async-start | bytes 1572864 | tf_op jit(solution)/shard_map/psum | solution.py:13
  8.0 6.0 collective-permute-start
  9.8 4.5 collective-permute-start.1
  14.1 1.9 copy-start.11
  15.6 1.0 copy-start
  18.7 4.2 copy-start.9
  19.0 8.8 %collective-permute-start.2 = (bf16[2,16,32,128]{3,2,1,0:T(8,128)(2,1)S(1)}, bf16[2,16,32,128]{3,2,1,0:T(8,128)(2,1)S(1)}, u32[]{:S(2)}, u32[]{:S(2)}) collective-permute-start(bf16[2,16,32,128]{3,2,1,0:T(8,128)(2,1)S(1)} %slice.195), channel_id=1, source_target_pairs={{0,8},{8,16},{16,24},{24,32},{32,40},{40,48},{48,56},{56,64},{64,7... | collective-permute-start | bytes 786440 | tf_op jit(solution)/shard_map/ppermute | solution.py:33
  27.8 1.2 copy-start.6
  29.1 60.8 %copy-start.1 = (bf16[1,4,16,32,128]{4,3,2,1,0:T(8,128)(2,1)S(1)}, bf16[1,4,16,32,128]{4,3,2,1,0:T(8,128)(2,1)}, u32[]{:S(2)}) copy-start(bf16[1,4,16,32,128]{4,3,2,1,0:T(8,128)(2,1)} %param.15) | copy-start | bytes 1572868
  87.0 0.6 copy-start.13
  89.8 14.9 %copy-start.14 = (f32[4,32]{1,0:T(4,128)S(1)}, f32[4,32]{1,0:T(4,128)}, u32[]{:S(2)}) copy-start(f32[4,32]{1,0:T(4,128)} %copy-done.13) | copy-start | bytes 1540
  89.8 14.9 %copy-start.15 = (f32[4,32]{1,0:T(4,128)S(1)}, f32[4,32]{1,0:T(4,128)}, u32[]{:S(2)}) copy-start(f32[4,32]{1,0:T(4,128)} %get-tuple-element.176) | copy-start | bytes 1540
  89.8 14.9 %copy-start.20 = (f32[4]{0:T(128)S(1)}, f32[4]{0:T(128)}, u32[]{:S(2)}) copy-start(f32[4]{0:T(128)} %fusion.122) | copy-start | bytes 52
  89.8 14.9 %copy-start.23 = (f32[4]{0:T(128)S(1)}, f32[4]{0:T(128)}, u32[]{:S(2)}) copy-start(f32[4]{0:T(128)} %fusion.121) | copy-start | bytes 52
  89.8 45.5 %copy-start.16 = (f32[4,128]{1,0:T(4,128)S(1)}, f32[4,128]{1,0:T(4,128)}, u32[]{:S(2)}) copy-start(f32[4,128]{1,0:T(4,128)} %mul.190) | copy-start | bytes 6148
  89.8 45.5 %copy-start.17 = (f32[4,128]{1,0:T(4,128)S(1)}, f32[4,128]{1,0:T(4,128)}, u32[]{:S(2)}) copy-start(f32[4,128]{1,0:T(4,128)} %sub.45) | copy-start | bytes 6148
  89.9 45.5 %copy-start.18 = (f32[128]{0:T(128)S(1)}, f32[128]{0:T(128)}, u32[]{:S(2)}) copy-start(f32[128]{0:T(128)} %param.13) | copy-start | bytes 1540
  89.9 45.5 %copy-start.19 = (f32[128]{0:T(128)S(1)}, f32[128]{0:T(128)}, u32[]{:S(2)}) copy-start(f32[128]{0:T(128)} %param.14) | copy-start | bytes 1540
  138.1 1.7 copy-start.21
  138.1 1.7 copy-start.22
  138.1 257.6 %copy-start.7 = (bf16[2,16,32,128]{3,2,1,0:T(8,128)(2,1)S(1)}, bf16[2,16,32,128]{3,2,1,0:T(8,128)(2,1)}, u32[]{:S(2)}) copy-start(bf16[2,16,32,128]{3,2,1,0:T(8,128)(2,1)} %copy-done.6) | copy-start | bytes 786436
  138.5 258.9 %collective-permute-start.3 = (bf16[2,16,32,128]{3,2,1,0:T(8,128)(2,1)S(1)}, bf16[2,16,32,128]{3,2,1,0:T(8,128)(2,1)S(1)}, u32[]{:S(2)}, u32[]{:S(2)}) collective-permute-start(bf16[2,16,32,128]{3,2,1,0:T(8,128)(2,1)S(1)} %slice.196), channel_id=1, source_target_pairs={{8,0},{16,8},{24,16},{32,24},{40,32},{48,40},{56,48},{64,56},{72,6... | collective-permute-start | bytes 786440 | tf_op jit(solution)/shard_map/ppermute | solution.py:33
  398.0 1.0 copy-start.5
  398.3 1.9 copy-start.12
  402.3 4.9 collective-permute-start.4
  404.1 3.3 collective-permute-start.5
  406.3 0.8 copy-start.8
  407.1 399.2 %all-reduce.17.cloned.1.call-start = ((), (), s32[]{:S(2)}) async-start(), calls=%async_computation | async-start | bytes 1572864 | tf_op jit(solution)/shard_map/psum | solution.py:13
  408.6 1.0 copy-start.2
  409.7 1.2 copy-start.3
  806.3 2.0 copy-start.10
Sparse Core Ops, SparseCore 0:
  407.2 55.1 all-reduce.18
  465.9 340.3 all-reduce.16
